TPU v7x, 32 devices: a whole 2x2x4 slice. The times are simulated.
32 devices in a mesh: width: 4 (over z), row: 4 (over y, core), src: 2 (over x).
Axes of the slice: x: 2, y: 2, z: 4, core: 2. Of those that a mesh axis runs over, the one named last changes fastest.
Arguments:
- query_rows: bfloat16 [1024, 8192], P('row', 'width'), may hold values from -150 to 150
- key_rows: bfloat16 [1024, 1024], P('src', 'width'), may hold values from -7 to 7
- value_rows: bfloat16 [1024, 1024], P('src'), may hold values from -6 to 6
- out_proj: bfloat16 [8192, 8192], P(('row', 'src'), 'width'), may hold values from -0.0625 to 0.0625
Outputs:
- share: float32 [1024, 1024], P('row', ('src', 'width'))
All inputs are finite; a program needn't handle non-finite values.
Results may differ from a plain program's by a relative error of at most 0.0014.
Values may be sent and summed in bfloat16 or wider, within the bound.
No kernel may reach another device: no remote copies, remote signals or barrier semaphores. Data moves between devices by JAX's collectives and lax.ppermute only.
A program may use at most 384 MiB of HBM per device.

v0:
```python
import math
import jax
import jax.numpy as jnp
from jax import lax
from jax.sharding import PartitionSpec as P

H = 64
KV = 8
HD = 128


def combined_all(shard, axis, combine):
    everything = jax.tree.map(lambda part: lax.all_gather(part, axis), shard)
    first = jax.tree.map(lambda part: part[0], everything)

    def step(k, so_far):
        return combine(so_far, jax.tree.map(lambda part: part[k], everything))

    return lax.fori_loop(1, lax.axis_size(axis), step, first)


def spread_positions(here_index, devices, piece_size):
    sender = jnp.arange(devices, dtype=jnp.int32)
    block_ids = sender * devices + (here_index - sender) % devices
    inner = jnp.arange(piece_size, dtype=jnp.int32)
    return (block_ids[:, None] * piece_size + inner[None, :]).reshape(-1)


def combine_stats(first, second):
    peak_one, mass_one = first
    peak_two, mass_two = second
    larger = jnp.maximum(peak_one, peak_two)
    return (larger, mass_one * jnp.exp(peak_one - larger) + mass_two * jnp.exp(peak_two - larger))


def body(query_rows, key_rows, value_rows, out_proj):
    row_devices = lax.axis_size("row")
    src_devices = lax.axis_size("src")
    here_row = lax.axis_index("row")
    here_src = lax.axis_index("src")
    row_count = query_rows.shape[0]
    col_count = key_rows.shape[0]
    piece_rows = row_count // row_devices
    piece_cols = col_count // src_devices
    group_size = H // KV
    stacked = jnp.roll(query_rows.reshape(row_devices, piece_rows, -1), here_row, axis=0)
    query_rows = lax.all_to_all(stacked, "row", split_axis=0, concat_axis=0, tiled=True).reshape(
        row_count, -1
    )
    key_stack = jnp.roll(key_rows.reshape(src_devices, piece_cols, -1), here_src, axis=0)
    value_stack = jnp.roll(value_rows.reshape(src_devices, piece_cols, -1), here_src, axis=0)
    key_stack, value_stack = (
        lax.all_to_all(key_stack, "src", split_axis=0, concat_axis=0, tiled=True),
        lax.all_to_all(value_stack, "src", split_axis=0, concat_axis=0, tiled=True),
    )
    key_rows = key_stack.reshape(col_count, -1)
    value_rows = value_stack.reshape(col_count, -1)
    row_pos = spread_positions(here_row, row_devices, piece_rows)
    col_pos = spread_positions(here_src, src_devices, piece_cols)
    local_heads = query_rows.shape[1] // HD
    local_kv = key_rows.shape[1] // HD
    queries = query_rows.reshape(row_count, local_kv, group_size, HD)
    key_heads = key_rows.reshape(col_count, local_kv, HD)
    scores = jnp.einsum("ikgd,jkd->kgij", queries, key_heads, preferred_element_type=jnp.float32)
    scores = scores.reshape(local_heads, row_count, col_count) / jnp.sqrt(jnp.float32(HD))
    causal = row_pos[:, None] >= col_pos[None, :]
    masked = jnp.where(causal, scores, jnp.float32(-1e30))
    row_peak = jnp.max(masked, axis=-1)
    row_mass = jnp.sum(jnp.where(causal, jnp.exp(masked - row_peak[..., None]), 0.0), axis=-1)
    row_peak, row_mass = combined_all((row_peak, row_mass), "src", combine_stats)
    weights = jnp.where(
        causal, jnp.exp(masked - row_peak[..., None]) / row_mass[..., None], 0.0
    ).astype(jnp.bfloat16)
    weights = lax.all_gather(weights, "width", axis=0, tiled=True)
    value_heads = value_rows.reshape(col_count, KV, HD)
    out_cols = out_proj.shape[1]
    proj_heads = out_proj.reshape(-1, HD, out_cols)
    portion = lax.all_gather(proj_heads, ("row", "src"), axis=0, tiled=True)
    head_count = portion.shape[0]
    head_ids = jnp.arange(head_count, dtype=jnp.int32)
    selector = (head_ids[:, None] // group_size == jnp.arange(KV, dtype=jnp.int32)[None, :]).astype(
        jnp.bfloat16
    )
    chosen = jnp.einsum(
        "hk,jkd->jhd", selector, value_heads, preferred_element_type=jnp.float32
    ).astype(jnp.bfloat16)
    images = jnp.einsum("jhd,hde->jhe", chosen, portion, preferred_element_type=jnp.float32).astype(
        jnp.bfloat16
    )
    row_block = math.gcd(row_count, 64)
    col_block = math.gcd(col_count, 32)
    col_steps = col_count // col_block
    turns = row_count // row_block * col_steps

    def tile(turn_index, running):
        row_start = turn_index // col_steps * row_block
        col_start = turn_index % col_steps * col_block
        row_slice = lax.dynamic_slice_in_dim(row_pos, row_start, row_block)
        col_slice = lax.dynamic_slice_in_dim(col_pos, col_start, col_block)

        def compute(unused):
            attend = lax.dynamic_slice(
                weights, (0, row_start, col_start), (H, row_block, col_block)
            )
            source_images = lax.dynamic_slice_in_dim(images, col_start, col_block, 0)
            contrib = jnp.einsum(
                "hij,jhe->ije", attend, source_images, preferred_element_type=jnp.float32
            )
            return jnp.sum(jnp.abs(contrib), axis=-1)

        def skipped(unused):
            return jnp.zeros((row_block, col_block), jnp.float32)

        result = lax.cond(jnp.max(row_slice) >= jnp.min(col_slice), compute, skipped, 0)
        return lax.dynamic_update_slice(running, result, (row_start, col_start))

    partial_value = lax.fori_loop(0, turns, tile, jnp.zeros((row_count, col_count), jnp.float32))
    partial_value = lax.all_to_all(
        lax.all_to_all(partial_value, "row", split_axis=0, concat_axis=0, tiled=True),
        "src",
        split_axis=1,
        concat_axis=1,
        tiled=True,
    )
    partial_value = jnp.roll(
        partial_value.reshape(row_devices, piece_rows, col_count), -here_row, axis=0
    ).reshape(row_count, col_count)
    partial_value = jnp.roll(
        partial_value.reshape(row_count, src_devices, piece_cols), -here_src, axis=1
    ).reshape(row_count, col_count)
    summed = lax.psum_scatter(partial_value, "width", scatter_dimension=1, tiled=True)
    totals = lax.psum(jnp.sum(summed, axis=1), ("width", "src"))
    position = (here_row * row_count + jnp.arange(row_count, dtype=jnp.int32) + 1).astype(
        jnp.float32
    )
    return position[:, None] * summed / totals[:, None]


def solution(mesh):
    placed = (P("row", "width"), P("src", "width"), P("src", None), P(("row", "src"), "width"))
    return jax.shard_map(
        body, mesh=mesh, in_specs=placed, out_specs=P("row", ("src", "width")), check_vma=False
    )
```

profile of v0, /device:TPU:0, one launch (start us, length us, event | category | flops | bytes accessed | tf_op | source)
XLA Modules:
  0.0 1261.2 jit_solution(17233729427972256463)
XLA Ops:
  23.1 13.2 %all-to-all-done.2 = bf16[4,64,2048]{2,1,0:T(8,128)(2,1)S(1)} async-done(((bf16[4,64,2048]{2,1,0:T(8,128)(2,1)}), bf16[4,64,2048]{2,1,0:T(8,128)(2,1)S(1)}, u32[]{:S(2)}, u32[]{:S(2)}) %all-to-all-start.2) | async-done | bytes 1048608 | tf_op jit(solution)/shard_map/all_to_all | solution.py:47
  51.9 9.3 copy.29
  73.0 11.0 all-to-all-done
  89.9 263.7 %all-gather.5.cloned.1.call-done = bf16[64,256,512]{2,1,0:T(8,128)(2,1)} async-done(((bf16[16,256,512]{2,1,0:T(8,128)(2,1)}), bf16[64,256,512]{2,1,0:T(8,128)(2,1)}) %all-gather.5.cloned.1.call-update) | async-done | bytes 16777232 | tf_op jit(solution)/shard_map/all_gather | solution.py:74
  353.6 56.4 %copy.31 = bf16[64,256,512]{0,1,2:T(8,128)(2,1)} copy(bf16[64,256,512]{2,1,0:T(8,128)(2,1)} %all-gather.5.cloned.1.call-done) | data formatting | bytes 33554432 | tf_op jit(solution)/shard_map/while | solution.py:117
  409.9 104.4 %all-gather.3.cloned.1.call-done = bf16[64,128,2048]{2,1,0:T(8,128)(2,1)} async-done(((bf16[8,128,2048]{2,1,0:T(8,128)(2,1)}), bf16[64,128,2048]{2,1,0:T(8,128)(2,1)}) %all-gather.3.cloned.1.call-update) | async-done | bytes 33554448 | tf_op jit(solution)/shard_map/all_gather | solution.py:78
  514.3 62.4 %convert_bitcast_fusion = bf16[512,64,2048]{2,0,1:T(8,128)(2,1)} fusion(bf16[64,128,2048]{2,1,0:T(8,128)(2,1)} %all-gather.3.cloned.1.call-done, bf16[512,64,128]{2,1,0:T(8,128)(2,1)} %convert_bitcast_fusion.1), kind=kOutput, calls=%fused_computation.7 | convolution fusion | flops 17246978048 | bytes 176160768 | tf_op jit(solution)/shard_map/jhd,hde->jhe/dot_general | solution.py:87
  576.7 111.2 %copy.30 = bf16[512,64,2048]{2,1,0:T(8,128)(2,1)} copy(bf16[512,64,2048]{2,0,1:T(8,128)(2,1)} %convert_bitcast_fusion) | data formatting | bytes 268435456 | tf_op jit(solution)/shard_map/while | solution.py:117
  688.0 449.8 %while.10 = (s32[]{:T(128)}, f32[256,512]{0,1:T(8,128)S(1)}, s32[256]{0:T(256)S(1)}, s32[512]{0:T(512)}, bf16[512,64,2048]{2,1,0:T(8,128)(2,1)}, /*index=5*/bf16...) while((s32[]{:T(128)}, f32[256,512]{0,1:T(8,128)S(1)}, ...), condition=%wide.region_8.9_spmd, body=%wide.region_2.8_spmd.sunk | while | flops 545257600 | bytes 8939890 | solution.py:117
  691.3 6.0 conditional.2
  770.1 6.0 conditional.2
  780.6 6.0 conditional.2
  791.1 6.0 conditional.2
  801.6 6.0 conditional.2
  812.0 6.0 conditional.2
  833.0 6.0 conditional.2
  843.5 6.0 conditional.2
  889.5 6.0 conditional.2
  899.5 6.0 conditional.2
  909.5 6.0 conditional.2
  1137.9 58.3 %all_to_all.33 = f32[4,64,512]{2,1,0:T(8,128)S(1)} all-to-all(f32[4,64,512]{2,1,0:T(8,128)S(1)} %bitcast.72), channel_id=1, replica_groups=mesh['width'=4,'row'=4,'src'=2] {'row'}, dimensions={0} | all-to-all | bytes 1048576 | tf_op jit(solution)/shard_map/all_to_all | solution.py:119
  1201.1 8.4 all-to-all-done.4
  1212.4 21.0 %reduce-scatter.2.cloned.1.call-done = f32[256,128]{1,0:T(8,128)} async-done(((f32[256,512]{1,0:T(8,128)}), f32[256,128]{1,0:T(8,128)}) %reduce-scatter.2.cloned.1.call-update) | async-done | bytes 131088 | tf_op jit(solution)/shard_map/reduce_scatter | solution.py:131
  1234.5 18.5 %psum.7 = f32[256]{0:T(256)S(1)} all-reduce(f32[256]{0:T(256)S(1)} %reduce_sum.30), channel_id=1, replica_groups=mesh['width'=4,'row'=4,'src'=2] {'width','src'}, use_global_device_ids=true, to_apply=%region_11.12 | all-reduce | flops 256 | bytes 2048 | tf_op jit(solution)/shard_map/psum | solution.py:132
  (365 shorter events, 545.8 us)
Async XLA Ops:
  8.3 10.1 all-to-all-start.1
  18.4 17.9 %all-to-all-start.2 = ((bf16[4,64,2048]{2,1,0:T(8,128)(2,1)}), bf16[4,64,2048]{2,1,0:T(8,128)(2,1)S(1)}, u32[]{:S(2)}, u32[]{:S(2)}) async-start(bf16[4,64,2048]{2,1,0:T(8,128)(2,1)} %fusion.8), calls=%async_computation.2 | async-start | bytes 2097152 | tf_op jit(solution)/shard_map/all_to_all | solution.py:47
  21.9 331.6 %all-gather.5.cloned.1.call-start = ((), (), s32[]{:S(2)}) async-start(), calls=%async_computation.7 | async-start | bytes 20971520 | tf_op jit(solution)/shard_map/all_gather | solution.py:74
  22.1 0.5 copy-start.3
  22.2 0.6 copy-start.2
  38.1 3.2 copy-start
  61.2 6.7 copy-start.1
  67.1 447.3 %all-gather.3.cloned.1.call-start = ((), (), s32[]{:S(2)}) async-start(), calls=%async_computation.6 | async-start | bytes 37748736 | tf_op jit(solution)/shard_map/all_gather | solution.py:78
  69.2 14.8 %all-to-all-start = ((bf16[2,256,1024]{2,1,0:T(8,128)(2,1)}), bf16[2,256,1024]{2,1,0:T(8,128)(2,1)S(1)}, u32[]{:S(2)}, u32[]{:S(2)}) async-start(bf16[2,256,1024]{2,1,0:T(8,128)(2,1)} %fusion.9), calls=%async_computation | async-start | bytes 2097152 | tf_op jit(solution)/shard_map/all_to_all | solution.py:54
  576.7 111.3 %copy-start.4 = (s32[256]{0:T(256)S(1)}, s32[256]{0:T(256)}, u32[]{:S(2)}) copy-start(s32[256]{0:T(256)} %copy-done.3) | copy-start | bytes 3076
  1197.4 12.1 all-to-all-start.4
  1201.1 32.3 %reduce-scatter.2.cloned.1.call-start = ((), (), s32[]{:S(2)}) async-start(), calls=%async_computation.8 | async-start | bytes 655360 | tf_op jit(solution)/shard_map/reduce_scatter | solution.py:131
Sparse Core Ops, SparseCore 0:
  67.2 286.3 all-gather.4
  355.4 158.8 all-gather.2
  1212.5 20.8 reduce-scatter.1
where the time goes:
time: 1270 us; the launch traced here: 1260 us
  waiting for transfers between devices  426 us (34%)
  matrix products  250 us (20%)
  local copies, waits for them, and re-layouts  241 us (19%)
  other arithmetic  151 us (12%)
  blocking collectives  85.6 us (7%)
  loops' own time  79.6 us (6%)
  starting transfers between devices  15.3 us (1%)
  between operations  13.3 us (1%)
    all_gather x1, waiting for transfers between devices, body(): weights = lax.all_gather(weights, 'width', axis=0, tiled=True)  264 us
    dot_general x30, matrix products, compute(): jnp.einsum('hij,jhe->ije', attend, source_images, preferred_element_type=...  180 us
    while x3, local copies, waits for them, and re-layouts, body(): lax.fori_loop(0, turns, tile, jnp.zeros((row_count, col_count), jnp.float...  168 us
    all_gather x1, waiting for transfers between devices, body(): portion = lax.all_gather(proj_heads, ('row', 'src'), axis=0, tiled=True)  104 us
    reduce_min x64, other arithmetic, tile(): jnp.min(col_slice)  90.4 us
    another operation x1, loops' own time, body(): lax.fori_loop(0, turns, tile, jnp.zeros((row_count, col_count), jnp.float...  78.1 us
    dot_general x1, matrix products, body(): jnp.einsum('jhd,hde->jhe', chosen, portion, preferred_element_type=jnp.fl...  62.4 us
    all_to_all x1, blocking collectives, body(): lax.all_to_all(partial_value, 'row', split_axis=0, concat_axis=0, tiled=T...  58.3 us
  transfers between devices with their start and end apart: 7, of which 7 were waited for; matrix products, arithmetic and copies ran while one was open for 5% of the time, Pallas kernels for 0%

commit v1 on v0

--- a/solution.py
+++ b/solution.py
@@ -71,7 +71,14 @@
     weights = jnp.where(
         causal, jnp.exp(masked - row_peak[..., None]) / row_mass[..., None], 0.0
     ).astype(jnp.bfloat16)
-    weights = lax.all_gather(weights, "width", axis=0, tiled=True)
+    ring = [weights]
+    for hop in range(3):
+        ring.append(lax.ppermute(ring[-1], "width", [(dev, (dev + 1) % 4) for dev in range(4)]))
+    weights = jnp.roll(
+        jnp.concatenate(ring[::-1], axis=0),
+        (lax.axis_index("width") + 1) * ring[0].shape[0],
+        axis=0,
+    )
     value_heads = value_rows.reshape(col_count, KV, HD)
     out_cols = out_proj.shape[1]
     proj_heads = out_proj.reshape(-1, HD, out_cols)

time: 1270 us -> 1210 us (0.953)
  waiting for transfers between devices: 426 us -> 317 us
  local copies, waits for them, and re-layouts: 241 us -> 279 us
    all_gather x1 -> x0, waiting for transfers between devices: 264 us -> none  [body(): weights = lax.all_gather(weights, 'width', axis=0, tiled=True)]
    ppermute x0 -> x3, waiting for transfers between devices: none -> 252 us  [body(): lax.ppermute(ring[-1], 'width', [(dev, (dev + 1) % 4) for dev in range(4)])]
    all_gather x1, waiting for transfers between devices: 104 us -> 0.01 us  [body(): portion = lax.all_gather(proj_heads, ('row', 'src'), axis=0, tiled=True)]
    unnamed x14 -> x28, local copies, waits for them, and re-layouts: 4.98 us -> 28.4 us
    dynamic_slice x0 -> x1, local copies, waits for them, and re-layouts: none -> 13.8 us  [body(): jnp.roll(jnp.concatenate(ring[::-1], axis=0), (lax.axis_index('width') +...]
  transfers between devices with their start and end apart: 7 -> 9, of which waited for: 7 -> 8; matrix products, arithmetic and copies ran while one was open for 5% -> 11% of each run, Pallas kernels for 0% -> 0%
where the time goes in v1:
time: 1210 us; the launch traced here: 1200 us
  waiting for transfers between devices  317 us (26%)
  local copies, waits for them, and re-layouts  279 us (23%)
  matrix products  253 us (21%)
  other arithmetic  158 us (13%)
  blocking collectives  87.4 us (7%)
  loops' own time  78.7 us (7%)
  starting transfers between devices  16.9 us (1%)
  between operations  13.7 us (1%)
    ppermute x3, waiting for transfers between devices, body(): lax.ppermute(ring[-1], 'width', [(dev, (dev + 1) % 4) for dev in range(4)])  252 us
    dot_general x30, matrix products, compute(): jnp.einsum('hij,jhe->ije', attend, source_images, preferred_element_type=...  180 us
    while x3, local copies, waits for them, and re-layouts, body(): lax.fori_loop(0, turns, tile, jnp.zeros((row_count, col_count), jnp.float...  168 us
    reduce_min x64, other arithmetic, tile(): jnp.min(col_slice)  90.8 us
    another operation x1, loops' own time, body(): lax.fori_loop(0, turns, tile, jnp.zeros((row_count, col_count), jnp.float...  77.3 us
    dot_general x1, matrix products, body(): jnp.einsum('jhd,hde->jhe', chosen, portion, preferred_element_type=jnp.fl...  62.3 us
    all_to_all x1, blocking collectives, body(): lax.all_to_all(partial_value, 'row', split_axis=0, concat_axis=0, tiled=T...  59.9 us
    dynamic_update_slice x64, local copies, waits for them, and re-layouts, tile(): return lax.dynamic_update_slice(running, result, (row_start, col_start))  56.5 us
  transfers between devices with their start and end apart: 9, of which 8 were waited for; matrix products, arithmetic and copies ran while one was open for 11% of the time, Pallas kernels for 0%

profile of v1, /device:TPU:0, one launch (start us, length us, event | category | flops | bytes accessed | tf_op | source)
XLA Modules:
  0.0 1203.6 jit_solution(3150298542242354196)
XLA Ops:
  24.0 24.2 %all-to-all-done.2 = bf16[4,64,2048]{2,1,0:T(8,128)(2,1)S(1)} async-done(((bf16[4,64,2048]{2,1,0:T(8,128)(2,1)}), bf16[4,64,2048]{2,1,0:T(8,128)(2,1)S(1)}, u32[]{:S(2)}, u32[]{:S(2)}) %all-to-all-start.2) | async-done | bytes 1048608 | tf_op jit(solution)/shard_map/all_to_all | solution.py:47
  53.2 9.3 copy.29
  80.9 90.8 %collective-permute-done = bf16[16,256,512]{2,1,0:T(8,128)(2,1)S(1)} collective-permute-done((bf16[16,256,512]{2,1,0:T(8,128)(2,1)S(1)}, bf16[16,256,512]{2,1,0:T(8,128)(2,1)S(1)}, u32[]{:S(2)}, u32[]{:S(2)}) %collective-permute-start) | collective-permute-done | bytes 4194336 | tf_op jit(solution)/shard_map/ppermute | solution.py:76
  173.7 91.7 %collective-permute-done.1 = bf16[16,256,512]{2,1,0:T(8,128)(2,1)} collective-permute-done((bf16[16,256,512]{2,1,0:T(8,128)(2,1)S(1)}, bf16[16,256,512]{2,1,0:T(8,128)(2,1)}, u32[]{:S(2)}, u32[]{:S(2)}) %collective-permute-start.1) | collective-permute-done | bytes 4194336 | tf_op jit(solution)/shard_map/ppermute | solution.py:76
  270.3 10.4 all-to-all-done
  286.6 69.7 %collective-permute-done.2 = bf16[16,256,512]{2,1,0:T(8,128)(2,1)} collective-permute-done((bf16[16,256,512]{2,1,0:T(8,128)(2,1)}, bf16[16,256,512]{2,1,0:T(8,128)(2,1)}, u32[]{:S(2)}, u32[]{:S(2)}) %collective-permute-start.2) | collective-permute-done | bytes 4194336 | tf_op jit(solution)/shard_map/ppermute | solution.py:76
  388.2 13.8 %constant_dynamic-slice_fusion = bf16[64,256,512]{2,1,0:T(8,128)(2,1)} fusion(bf16[128,256,512]{2,1,0:T(8,128)(2,1)} %constant_dynamic-update-slice_fusion, s32[]{:T(128)S(6)} %select_n.184), kind=kLoop, calls=%fused_computation.52 | loop fusion | bytes 33554436 | tf_op jit(solution)/shard_map/jit(_roll_dynamic)/dynamic_slice | solution.py:77
  402.0 56.4 %copy.31 = bf16[64,256,512]{0,1,2:T(8,128)(2,1)} copy(bf16[64,256,512]{2,1,0:T(8,128)(2,1)} %constant_dynamic-slice_fusion) | data formatting | bytes 33554432 | tf_op jit(solution)/shard_map/while | solution.py:124
  458.4 62.3 %convert_bitcast_fusion = bf16[512,64,2048]{2,0,1:T(8,128)(2,1)} fusion(bf16[64,128,2048]{2,1,0:T(8,128)(2,1)} %all-gather.2.cloned.1.call-done, bf16[512,64,128]{2,1,0:T(8,128)(2,1)} %convert_bitcast_fusion.1), kind=kOutput, calls=%fused_computation.7 | convolution fusion | flops 17246978048 | bytes 176160768 | tf_op jit(solution)/shard_map/jhd,hde->jhe/dot_general | solution.py:94
  520.7 111.3 %copy.30 = bf16[512,64,2048]{2,1,0:T(8,128)(2,1)} copy(bf16[512,64,2048]{2,0,1:T(8,128)(2,1)} %convert_bitcast_fusion) | data formatting | bytes 268435456 | tf_op jit(solution)/shard_map/while | solution.py:124
  632.1 449.3 %while.10 = (s32[]{:T(128)}, f32[256,512]{0,1:T(8,128)S(1)}, s32[256]{0:T(256)S(1)}, s32[512]{0:T(512)}, bf16[512,64,2048]{2,1,0:T(8,128)(2,1)}, /*index=5*/bf16...) while((s32[]{:T(128)}, f32[256,512]{0,1:T(8,128)S(1)}, ...), condition=%wide.region_8.9_spmd, body=%wide.region_2.8_spmd.sunk | while | flops 545257600 | bytes 8939898 | solution.py:124
  645.5 6.0 conditional.2
  714.1 6.0 conditional.2
  724.5 6.0 conditional.2
  735.0 6.0 conditional.2
  745.5 6.0 conditional.2
  756.0 6.0 conditional.2
  766.4 6.0 conditional.2
  776.9 6.0 conditional.2
  787.4 6.0 conditional.2
  1081.5 59.9 %all_to_all.33 = f32[4,64,512]{2,1,0:T(8,128)S(1)} all-to-all(f32[4,64,512]{2,1,0:T(8,128)S(1)} %bitcast.74), channel_id=1, replica_groups=mesh['width'=4,'row'=4,'src'=2] {'row'}, dimensions={0} | all-to-all | bytes 1048576 | tf_op jit(solution)/shard_map/all_to_all | solution.py:126
  1146.2 7.8 all-to-all-done.4
  1156.9 18.6 %reduce-scatter.2.cloned.1.call-done = f32[256,128]{1,0:T(8,128)} async-done(((f32[256,512]{1,0:T(8,128)}), f32[256,128]{1,0:T(8,128)}) %reduce-scatter.2.cloned.1.call-update) | async-done | bytes 131088 | tf_op jit(solution)/shard_map/reduce_scatter | solution.py:138
  1176.5 18.6 %psum.7 = f32[256]{0:T(256)S(1)} all-reduce(f32[256]{0:T(256)S(1)} %reduce_sum.30), channel_id=1, replica_groups=mesh['width'=4,'row'=4,'src'=2] {'width','src'}, use_global_device_ids=true, to_apply=%region_11.12 | all-reduce | flops 256 | bytes 2048 | tf_op jit(solution)/shard_map/psum | solution.py:139
  (386 shorter events, 593.8 us)
Async XLA Ops:
  6.5 451.9 %all-gather.2.cloned.1.call-start = ((), (), s32[]{:S(2)}) async-start(), calls=%async_computation.6 | async-start | bytes 37748736 | tf_op jit(solution)/shard_map/all_gather | solution.py:85
  9.0 10.1 all-to-all-start.1
  19.1 29.0 %all-to-all-start.2 = ((bf16[4,64,2048]{2,1,0:T(8,128)(2,1)}), bf16[4,64,2048]{2,1,0:T(8,128)(2,1)S(1)}, u32[]{:S(2)}, u32[]{:S(2)}) async-start(bf16[4,64,2048]{2,1,0:T(8,128)(2,1)} %fusion.8), calls=%async_computation.2 | async-start | bytes 2097152 | tf_op jit(solution)/shard_map/all_to_all | solution.py:47
  22.9 0.5 copy-start.5
  23.0 0.6 copy-start.4
  62.5 14.2 %copy-start = (f32[16,256,512]{2,1,0:T(8,128)S(1)}, f32[16,256,512]{2,1,0:T(8,128)}, u32[]{:S(2)}) copy-start(f32[16,256,512]{2,1,0:T(8,128)} %copy.29) | copy-start | bytes 25165828
  67.7 197.7 %copy-start.3 = (bf16[512,1024]{1,0:T(8,128)(2,1)S(1)}, bf16[512,1024]{1,0:T(8,128)(2,1)}, u32[]{:S(2)}) copy-start(bf16[512,1024]{1,0:T(8,128)(2,1)} %param.10) | copy-start | bytes 3145732
  78.9 92.8 %collective-permute-start = (bf16[16,256,512]{2,1,0:T(8,128)(2,1)S(1)}, bf16[16,256,512]{2,1,0:T(8,128)(2,1)S(1)}, u32[]{:S(2)}, u32[]{:S(2)}) collective-permute-start(bf16[16,256,512]{2,1,0:T(8,128)(2,1)S(1)} %select_convert_fusion), channel_id=1, source_target_pairs={{0,8},{8,16},{16,24},{24,0},{1,9},{9,17},{17,25},{25,1},{2,10},{10... | collective-permute-start | bytes 12582920 | tf_op jit(solution)/shard_map/ppermute | solution.py:76
  171.7 2.0 copy-start.1
  173.7 91.7 %collective-permute-start.1 = (bf16[16,256,512]{2,1,0:T(8,128)(2,1)S(1)}, bf16[16,256,512]{2,1,0:T(8,128)(2,1)}, u32[]{:S(2)}, u32[]{:S(2)}) collective-permute-start(bf16[16,256,512]{2,1,0:T(8,128)(2,1)S(1)} %collective-permute-done), channel_id=1, source_target_pairs={{0,8},{8,16},{16,24},{24,0},{1,9},{9,17},{17,25},{25,1},{2,10},{10... | collective-permute-start | bytes 12582920 | tf_op jit(solution)/shard_map/ppermute | solution.py:76
  265.4 91.0 %collective-permute-start.2 = (bf16[16,256,512]{2,1,0:T(8,128)(2,1)}, bf16[16,256,512]{2,1,0:T(8,128)(2,1)}, u32[]{:S(2)}, u32[]{:S(2)}) collective-permute-start(bf16[16,256,512]{2,1,0:T(8,128)(2,1)} %collective-permute-done.1), channel_id=1, source_target_pairs={{0,8},{8,16},{16,24},{24,0},{1,9},{9,17},{17,25},{25,1},{2,10},{10... | collective-permute-start | bytes 12582920 | tf_op jit(solution)/shard_map/ppermute | solution.py:76
  266.7 14.0 %all-to-all-start = ((bf16[2,256,1024]{2,1,0:T(8,128)(2,1)}), bf16[2,256,1024]{2,1,0:T(8,128)(2,1)S(1)}, u32[]{:S(2)}, u32[]{:S(2)}) async-start(bf16[2,256,1024]{2,1,0:T(8,128)(2,1)} %fusion.9), calls=%async_computation | async-start | bytes 2097152 | tf_op jit(solution)/shard_map/all_to_all | solution.py:54
  286.6 79.0 %copy-start.2 = (bf16[16,256,512]{2,1,0:T(8,128)(2,1)S(1)}, bf16[16,256,512]{2,1,0:T(8,128)(2,1)}, u32[]{:S(2)}) copy-start(bf16[16,256,512]{2,1,0:T(8,128)(2,1)} %copy-done.1) | copy-start | bytes 12582916
  361.0 7.2 slice-start
  365.7 3.7 slice-start.1
  520.7 111.3 %copy-start.6 = (s32[256]{0:T(256)S(1)}, s32[256]{0:T(256)}, u32[]{:S(2)}) copy-start(s32[256]{0:T(256)} %copy-done.5) | copy-start | bytes 3076
  1142.6 11.4 all-to-all-start.4
  1146.1 29.4 %reduce-scatter.2.cloned.1.call-start = ((), (), s32[]{:S(2)}) async-start(), calls=%async_computation.7 | async-start | bytes 655360 | tf_op jit(solution)/shard_map/reduce_scatter | solution.py:138
Sparse Core Ops, SparseCore 0:
  9.2 173.5 all-gather.1
  1157.0 18.4 reduce-scatter.1
